TPU v7x, 32 devices: a whole 2x2x4 slice. The times are simulated.
32 devices in a mesh: pair: 4 (over y, x), vtile: 8 (over z, core).
Axes of the slice: x: 2, y: 2, z: 4, core: 2. Of those that a mesh axis runs over, the one named last changes fastest.
Arguments:
- amplitudes: bfloat16 [32, 512, 512], P(('pair', 'vtile')), may hold values from -1.1953125 to 1.1953125
- factors: bfloat16 [512, 512, 2048], P('vtile', 'pair'), may hold values from -0.125 to 0.125
- pair_list: int32 [32, 2], P(('pair', 'vtile')), may hold values from 0 to 127
- window_offsets: int32 [2], replicated, may hold values from 0 to 511
- occupied_energy: float32 [128], replicated, may hold values from -3 to -0.5
- virtual_energy: float32 [512], replicated, may hold values from 0.5 to 4
Outputs:
- residual: float32 [32, 2, 512], P(('pair', 'vtile'))
- update: float32 [32, 2, 512], P(('pair', 'vtile'))
All inputs are finite; a program needn't handle non-finite values.
Results may differ from a plain program's by a relative error of at most 0.0029.
Values may be sent and summed in bfloat16 or wider, within the bound.
A program may use at most 128 MiB of HBM per device.

v0:
```python
import jax
import jax.numpy as jnp
from jax import lax
from jax.sharding import PartitionSpec as P


def broadcast(x, axis, root):
    mine = lax.axis_index(axis) == root
    return lax.psum(jnp.where(mine, x, jnp.zeros_like(x)), axis)


def lookup(table, indices):
    positions = jnp.arange(table.shape[0], dtype=jnp.int32)
    return jnp.sum(jnp.where(positions[None, :] == indices[:, None], table[None, :], 0.0), axis=1)


def local(amplitudes, factors, pair_list, window_offsets, occupied_energy, virtual_energy):
    pair_count = lax.axis_size("pair")
    tile_count = lax.axis_size("vtile")
    row_count, col_count, aux_count = factors.shape
    window_count = window_offsets.shape[0]
    local_pairs, virt_count = (amplitudes.shape[0], amplitudes.shape[1])
    total_pairs = local_pairs * pair_count * tile_count
    local_rows = window_offsets % row_count
    owners = window_offsets // row_count
    picked = jnp.stack(
        [
            lax.dynamic_index_in_dim(factors, local_rows[slot_index], 0, keepdims=False)
            for slot_index in range(window_count)
        ]
    )
    columns = lax.all_gather(picked, "pair", axis=1, tiled=True)
    arows = jnp.stack(
        [
            broadcast(columns[slot_index], "vtile", owners[slot_index])
            for slot_index in range(window_count)
        ]
    )
    integrals = jnp.einsum(
        "acq,bdq->abcd", arows, factors, preferred_element_type=jnp.float32
    ).astype(jnp.bfloat16)
    kernel = integrals.reshape(window_count * row_count, virt_count * col_count)
    mine = lax.all_to_all(amplitudes, "pair", split_axis=2, concat_axis=0, tiled=True)
    section = lax.all_gather(mine, "vtile", axis=0, tiled=True)
    row_total = section.shape[0]
    flat = section.reshape(row_total, virt_count * col_count)
    folded = lax.dot_general(
        flat, kernel, (((1,), (1,)), ((), ())), preferred_element_type=jnp.float32
    )
    partial_value = (
        folded.reshape(tile_count, pair_count, local_pairs, window_count * row_count)
        .transpose(1, 0, 2, 3)
        .reshape(total_pairs, window_count * row_count)
    )
    summed = lax.psum_scatter(partial_value, "pair", scatter_dimension=0, tiled=True)
    summed = summed.reshape(tile_count * local_pairs, window_count, row_count)
    residual = lax.all_to_all(summed, "vtile", split_axis=0, concat_axis=2, tiled=True)
    occupied_sum = lookup(occupied_energy, pair_list[:, 0]) + lookup(
        occupied_energy, pair_list[:, 1]
    )
    window_energy = lookup(virtual_energy, window_offsets)
    denominator = (
        window_energy[None, :, None] + virtual_energy[None, None, :] - occupied_sum[:, None, None]
    )
    update = residual / denominator
    return (residual, update)


def solution(mesh):
    return jax.shard_map(
        local,
        mesh=mesh,
        in_specs=(
            P(("pair", "vtile"), None, None),
            P("vtile", "pair", None),
            P(("pair", "vtile"), None),
            P(),
            P(),
            P(),
        ),
        out_specs=(P(("pair", "vtile"), None, None), P(("pair", "vtile"), None, None)),
        check_vma=False,
    )
```

profile of v0, /device:TPU:0, one launch (start us, length us, event | category | flops | bytes accessed | tf_op | source)
XLA Modules:
  0.0 277.9 jit_solution(16092452196197665802)
XLA Ops:
  7.2 0.7 and_select_fusion.1
  7.9 0.6 fusion.17
  12.2 1.3 constant_dynamic-slice_fusion.2
  13.5 1.1 pad_maximum_fusion
  16.0 54.1 %all-gather.4.cloned.1.call-done = bf16[2,512,2048]{2,1,0:T(8,128)(2,1)} async-done(((bf16[2,128,2048]{2,1,0:T(8,128)(2,1)}), bf16[2,512,2048]{2,1,0:T(8,128)(2,1)}) %all-gather.4.cloned.1.call-update) | async-done | bytes 4194320 | tf_op jit(solution)/shard_map/all_gather | solution.py:32
  70.1 4.5 %slice_select_fusion.1 = (bf16[1,512,2048]{2,1,0:T(8,128)(2,1)}, bf16[1,512,2048]{2,1,0:T(8,128)(2,1)}) fusion(bf16[2,512,2048]{2,1,0:T(8,128)(2,1)} %all-gather.4.cloned.1.call-done, pred[]{:T(512)S(6)} %eq.43, pred[]{:T(512)S(6)} %eq.44), kind=kLoop, calls=%fused_computation.12 | loop fusion | flops 2097152 | bytes 8388610 | tf_op jit(solution)/shard_map/jit(_where)/select_n | solution.py:9
  74.6 1.0 copy-done
  75.6 0.9 copy.21
  77.0 3.9 %reduce.4 = bf16[512,512]{1,0:T(8,128)(2,1)S(1)} reduce(bf16[512,1,512]{2,1,0:T(2,128)(2,1)S(1)} %bitcast.50, bf16[]{:T(256)} %broadcast.101), dimensions={1}, to_apply=%bitcast.43.reduce_sub_computation | reduce | bytes 1048578
  81.2 11.0 %all_to_all.36 = bf16[4,2,32768]{2,1,0:T(2,128)(2,1)S(1)} all-to-all(bf16[4,2,32768]{2,1,0:T(2,128)(2,1)S(1)} %reshape.120), channel_id=1, replica_groups=mesh['pair'=4,'vtile'=8] {'pair'}, dimensions={0} | all-to-all | bytes 1048576 | tf_op jit(solution)/shard_map/all_to_all | solution.py:43
  92.9 1.0 copy.22
  94.0 0.6 dynamic-slice
  95.3 0.6 fusion.16
  96.1 75.2 %all-reduce.4.cloned.1.call-done = (bf16[1,512,2048]{2,1,0:T(8,128)(2,1)}, bf16[1,512,2048]{2,1,0:T(8,128)(2,1)}) async-done(((bf16[1,512,2048]{2,1,0:T(8,128)(2,1)}, bf16[1,512,2048]{2,1,0:T(8,128)(2,1)}), (bf16[1,512,2048]{2,1,0:T(8,128)(2,1)}, bf16[1,512,2048]{2,1,0:T(8,128)(2,1)})) %all-reduce.4.cloned.1.call-update) | async-done | bytes 4194320 | tf_op jit(solution)/shard_map/psum | solution.py:9
  171.2 41.1 %fusion.5 = bf16[2,512,64,128]{3,1,2,0:T(8,128)(2,1)} fusion(bf16[64,128,2048]{2,1,0:T(8,128)(2,1)} %param.7, bf16[1,512,2048]{2,1,0:T(8,128)(2,1)} %get-tuple-element.4, bf16[1,512,2048]{2,1,0:T(8,128)(2,1)} %get-tuple-element.5), kind=kOutput, calls=%fused_computation.5 | convolution fusion | flops 34376515584 | bytes 54525952 | tf_op jit(solution)/shard_map/acq,bdq->abcd/dot_general | solution.py:39
  212.4 7.4 %all-gather.6.cloned.1.call-done = bf16[32,1,512,128]{3,2,1,0:T(8,128)(2,1)} async-done(((bf16[4,1,512,128]{3,2,1,0:T(8,128)(2,1)}), bf16[32,1,512,128]{3,2,1,0:T(8,128)(2,1)}) %all-gather.6.cloned.1.call-update) | async-done | bytes 4194320 | tf_op jit(solution)/shard_map/all_gather | solution.py:44
  219.8 24.0 %fusion.2 = f32[128,32]{0,1:T(8,128)S(1)} fusion(bf16[16,8,512,128]{3,2,1,0:T(8,128)(2,1)} %bitcast.56, bf16[4,8,512,128]{3,2,1,0:T(8,128)(2,1)} %bitcast.55), kind=kOutput, calls=%fused_computation.2 | convolution fusion | flops 536870912 | bytes 20987904 | tf_op jit(solution)/shard_map/dot_general | solution.py:47
  243.8 16.0 %all-reduce = f32[32,128]{1,0:T(8,128)S(1)} all-reduce(f32[32,128]{1,0:T(8,128)S(1)} %bitcast.52), channel_id=3, replica_groups=mesh['pair'=4,'vtile'=8] {'pair'}, use_global_device_ids=true, to_apply=%region_2.3.clone | all-reduce | flops 4096 | bytes 32768
  259.9 0.7 reshape.122
  260.6 3.3 %all-to-all-start.1 = ((f32[8,1,128]{2,1,0:T(1,128)}), f32[8,1,128]{2,1,0:T(1,128)S(1)}, u32[]{:S(2)}, u32[]{:S(2)}) async-start(f32[8,1,128]{2,1,0:T(1,128)} %reshape.122), calls=%async_computation.1 | async-start | bytes 8192 | tf_op jit(solution)/shard_map/all_to_all | solution.py:57
  263.9 2.0 fusion.14
  267.1 2.2 all-to-all-done.1
  269.8 0.7 reduce.5
  270.7 0.7 subtract_divide_fusion
  (31 shorter events, 2.7 us)
Async XLA Ops:
  7.2 62.9 %all-gather.4.cloned.1.call-start = ((), (), s32[]{:S(2)}) async-start(), calls=%async_computation.2 | async-start | bytes 5242880 | tf_op jit(solution)/shard_map/all_gather | solution.py:32
  14.6 156.6 %all-reduce.4.cloned.1.call-start = ((), (), s32[]{:S(2)}) async-start(), calls=%async_computation.4 | async-start | bytes 8388608 | tf_op jit(solution)/shard_map/psum | solution.py:9
  74.5 1.0 copy-start
  74.6 145.2 %all-gather.6.cloned.1.call-start = ((), (), s32[]{:S(2)}) async-start(), calls=%async_computation.3 | async-start | bytes 4718592 | tf_op jit(solution)/shard_map/all_gather | solution.py:44
  77.0 17.0 %copy-start.6 = (u32[32]{0:T(128)S(1)}, u32[32]{0:T(128)}, u32[]{:S(2)}) copy-start(u32[32]{0:T(128)} %constant.46) | copy-start | bytes 388
  77.0 18.3 %copy-start.3 = (s32[1,2]{1,0:T(1,128)S(1)}, s32[1,2]{1,0:T(1,128)}, u32[]{:S(2)}) copy-start(s32[1,2]{1,0:T(1,128)} %param.8) | copy-start | bytes 28
  77.0 18.9 %copy-start.2 = (f32[512]{0:T(512)S(1)}, f32[512]{0:T(512)}, u32[]{:S(2)}) copy-start(f32[512]{0:T(512)} %param.11) | copy-start | bytes 6148
  77.0 18.9 %copy-start.5 = (s32[2]{0:T(128)S(1)}, s32[2]{0:T(128)}, u32[]{:S(2)}) copy-start(s32[2]{0:T(128)} %param.9) | copy-start | bytes 28
  219.8 44.1 %copy-start.4 = (f32[128]{0:T(128)S(1)}, f32[128]{0:T(128)}, u32[]{:S(2)}) copy-start(f32[128]{0:T(128)} %param.10) | copy-start | bytes 1540
  260.6 8.8 %all-to-all-start.1 = ((f32[8,1,128]{2,1,0:T(1,128)}), f32[8,1,128]{2,1,0:T(1,128)S(1)}, u32[]{:S(2)}, u32[]{:S(2)}) async-start(f32[8,1,128]{2,1,0:T(1,128)} %reshape.122), calls=%async_computation.1 | async-start | bytes 8192 | tf_op jit(solution)/shard_map/all_to_all | solution.py:57
  270.7 0.7 copy-start.1
Sparse Core Ops, SparseCore 0:
  14.7 55.2 all-gather.3
  74.7 96.5 all-reduce.3
  172.8 46.8 all-gather.5
where the time goes:
time: 278 us
  waiting for transfers between devices  139 us (50%)
  matrix products  65.2 us (23%)
  blocking collectives  27 us (10%)
  between operations  20.8 us (7%)
  other arithmetic  13.6 us (5%)
  local copies, waits for them, and re-layouts  8.95 us (3%)
  starting transfers between devices  3.43 us (1%)
    psum x1, waiting for transfers between devices, broadcast(): return lax.psum(jnp.where(mine, x, jnp.zeros_like(x)), axis)  75.2 us
    all_gather x1, waiting for transfers between devices, local(): columns = lax.all_gather(picked, 'pair', axis=1, tiled=True)  54.1 us
    dot_general x1, matrix products, local(): jnp.einsum('acq,bdq->abcd', arows, factors, preferred_element_type=jnp.fl...  41.1 us
    dot_general x1, matrix products, local(): lax.dot_general(flat, kernel, (((1,), (1,)), ((), ())), preferred_element...  24 us
    unnamed x1, blocking collectives  16 us
    all_to_all x1, blocking collectives, local(): lax.all_to_all(amplitudes, 'pair', split_axis=2, concat_axis=0, tiled=True)  11 us
    all_gather x1, waiting for transfers between devices, local(): section = lax.all_gather(mine, 'vtile', axis=0, tiled=True)  7.4 us
  transfers between devices with their start and end apart: 4, of which 4 were waited for; matrix products, arithmetic and copies ran while one was open for 19% of the time, Pallas kernels for 0%

commit v1 on v0

v1 whole, which is shorter than its diff:
```python
import functools

import jax
import jax.numpy as jnp
from jax import lax
from jax.experimental import pallas as pl
from jax.experimental.pallas import tpu as pltpu
from jax.sharding import PartitionSpec as P

MESH = pl.DeviceIdType.MESH


def lookup(table, indices):
    positions = jnp.arange(table.shape[0], dtype=jnp.int32)
    return jnp.sum(jnp.where(positions[None, :] == indices[:, None], table[None, :], 0.0), axis=1)


def spread_kernel(
    pair_count, tile_count, sub,
    rows_ref, amp_ref, full_ref, mine_ref,
    core_buf, own_buf, up_buf, down_buf, up_out, down_out,
    core_sems, up_sems, down_sems, peer_sems, fwd_sems, amp_sems, local_sem,
):
    p = lax.axis_index("pair")
    t = lax.axis_index("vtile")
    core = lax.rem(t, 2)
    stage = t // 2
    stages = tile_count // 2
    window, cols, aux = rows_ref.shape
    half = aux // 2
    mate = (p, stage * 2 + (1 - core))
    above = (p, t + 2)
    below = (p, t - 2)
    peers = [(lax.rem(p + j, pair_count), t) for j in range(1, pair_count)]
    sources = [lax.rem(p + pair_count - j, pair_count) for j in range(1, pair_count)]

    barrier = pltpu.get_barrier_semaphore()
    around = [(p, lax.rem(t + 2, tile_count)), (p, lax.rem(t + tile_count - 2, tile_count))]
    for device in [mate] + peers + around:
        pl.semaphore_signal(barrier, inc=1, device_id=device, device_id_type=MESH)
    pl.semaphore_wait(barrier, pair_count + 2)

    mine_lanes = pl.ds(pl.multiple_of(core * half, half), half)
    mate_lanes = pl.ds(pl.multiple_of((1 - core) * half, half), half)
    chunks = [(k, pl.ds(s * sub, sub)) for k in range(window) for s in range(cols // sub)]
    count = len(chunks)

    def remote(src, dst, sems, index, device):
        return pltpu.make_async_remote_copy(
            src_ref=src, dst_ref=dst, send_sem=sems.at[(0,) + index], recv_sem=sems.at[(1,) + index],
            device_id=device, device_id_type=MESH,
        )

    def core_copy(h):
        k, rows = chunks[h]
        return remote(rows_ref.at[k, rows, mate_lanes], core_buf.at[k, rows], core_sems, (h,), mate)

    def up_copy(h):
        k, rows = chunks[h]
        return remote(up_out.at[k, rows], up_buf.at[k, rows], up_sems, (h,), above)

    def down_copy(h):
        k, rows = chunks[h]
        return remote(down_out.at[k, rows], down_buf.at[k, rows], down_sems, (h,), below)

    def peer_copy(h, j):
        k, rows = chunks[h]
        place = full_ref.at[k, p, rows, mine_lanes]
        return remote(place, place, peer_sems, (j, h), peers[j])

    def fwd_copy(h, j):
        k, rows = chunks[h]
        source = p if j == pair_count - 1 else sources[j]
        place = full_ref.at[k, source, rows, mine_lanes]
        return remote(place, place, fwd_sems, (j, h), mate)

    def amp_copy(j):
        return remote(amp_ref.at[peers[j][0]], mine_ref.at[p], amp_sems, (j,), peers[j])

    for h in range(count):
        core_copy(h).start()
    for j in range(pair_count - 1):
        amp_copy(j).start()
    keep = pltpu.make_async_copy(amp_ref.at[p], mine_ref.at[p], local_sem)
    keep.start()

    def combine(h):
        k, rows = chunks[h]
        core_copy(h).wait_recv()
        own_buf[k, rows, :] = rows_ref[k, rows, mine_lanes] + core_buf[k, rows, :]

        @pl.when(stage == 0)
        def _():
            up_out[k, rows, :] = own_buf[k, rows, :]
            up_copy(h).start()

        @pl.when(stage == stages - 1)
        def _():
            down_out[k, rows, :] = own_buf[k, rows, :]
            down_copy(h).start()

    def go_up(h):
        k, rows = chunks[h]

        @pl.when(stage > 0)
        def _():
            up_copy(h).wait_recv()

            @pl.when(stage < stages - 1)
            def _():
                up_out[k, rows, :] = own_buf[k, rows, :] + up_buf[k, rows, :]
                up_copy(h).start()

    def go_down(h):
        k, rows = chunks[h]

        @pl.when(stage < stages - 1)
        def _():
            down_copy(h).wait_recv()

            @pl.when(stage > 0)
            def _():
                down_out[k, rows, :] = own_buf[k, rows, :] + down_buf[k, rows, :]
                down_copy(h).start()

    def finish(h):
        k, rows = chunks[h]

        @pl.when(stage == 0)
        def _():
            full_ref[k, p, rows, mine_lanes] = own_buf[k, rows, :] + down_buf[k, rows, :]

        @pl.when(stage == stages - 1)
        def _():
            full_ref[k, p, rows, mine_lanes] = own_buf[k, rows, :] + up_buf[k, rows, :]

        @pl.when(jnp.logical_and(stage > 0, stage < stages - 1))
        def _():
            full_ref[k, p, rows, mine_lanes] = (
                own_buf[k, rows, :] + up_buf[k, rows, :] + down_buf[k, rows, :]
            )

        for j in range(pair_count - 1):
            peer_copy(h, j).start()
        fwd_copy(h, pair_count - 1).start()

    def forward(h):
        for j in range(pair_count - 1):
            peer_copy(h, j).wait_recv()
            fwd_copy(h, j).start()

    for h in range(count):
        combine(h)
    lag = 3
    for step in range(count + lag):
        if step < count:
            go_up(step)
            go_down(step)
            finish(step)
        if step >= lag:
            forward(step - lag)
    for h in range(count):
        core_copy(h).wait_send()

        @pl.when(stage < stages - 1)
        def _():
            up_copy(h).wait_send()

        @pl.when(stage > 0)
        def _():
            down_copy(h).wait_send()

        for j in range(pair_count - 1):
            peer_copy(h, j).wait_send()
        for j in range(pair_count):
            fwd_copy(h, j).wait()
    for j in range(pair_count - 1):
        amp_copy(j).wait()
    keep.wait()


def spread(picked, amp, pair_count, tile_count):
    window, cols, aux = picked.shape
    half = aux // 2
    sub = max(16, cols // 4)
    count = window * cols // sub
    block = pltpu.VMEM((window, cols, half), picked.dtype)
    dma = pltpu.SemaphoreType.DMA
    vmem = pl.BlockSpec(memory_space=pltpu.VMEM)
    return pl.pallas_call(
        functools.partial(spread_kernel, pair_count, tile_count, sub),
        out_shape=(
            jax.ShapeDtypeStruct((window, pair_count, cols, aux), picked.dtype),
            jax.ShapeDtypeStruct(amp.shape, amp.dtype),
        ),
        in_specs=[vmem, vmem],
        out_specs=(vmem, vmem),
        scratch_shapes=[block] * 6
        + [
            dma((2, count)), dma((2, count)), dma((2, count)),
            dma((2, pair_count - 1, count)), dma((2, pair_count, count)),
            dma((2, pair_count - 1)), dma,
        ],
        compiler_params=pltpu.CompilerParams(
            collective_id=0, has_side_effects=True, vmem_limit_bytes=32 * 1024 * 1024
        ),
    )(picked, amp)


def settle_kernel(pair_count, tile_count, part_ref, sum_ref, inbox, sems, local_sem):
    p = lax.axis_index("pair")
    t = lax.axis_index("vtile")
    total = pair_count * tile_count
    me = p * tile_count + t
    barrier = pltpu.get_barrier_semaphore()

    def place(offset):
        other = lax.rem(me + offset, total)
        return other // tile_count, lax.rem(other, tile_count)

    for offset in range(1, total):
        pl.semaphore_signal(barrier, inc=1, device_id=place(offset), device_id_type=MESH)
    pl.semaphore_wait(barrier, total - 1)

    def copy(offset):
        there = place(offset)
        return pltpu.make_async_remote_copy(
            src_ref=part_ref.at[there[1], there[0]], dst_ref=inbox.at[p, t],
            send_sem=sems.at[0, offset], recv_sem=sems.at[1, offset],
            device_id=there, device_id_type=MESH,
        )

    for offset in range(1, total):
        copy(offset).start()
    keep = pltpu.make_async_copy(part_ref.at[t, p], inbox.at[p, t], local_sem)
    keep.start()
    keep.wait()
    for offset in range(1, total):
        copy(offset).wait()
    added = inbox[0]
    for source in range(1, pair_count):
        added = added + inbox[source]
    sum_ref[...] = added


def settle(part):
    tile_count, pair_count, local_pairs, width = part.shape
    total = tile_count * pair_count
    vmem = pl.BlockSpec(memory_space=pltpu.VMEM)
    return pl.pallas_call(
        functools.partial(settle_kernel, pair_count, tile_count),
        out_shape=jax.ShapeDtypeStruct((tile_count, local_pairs, width), part.dtype),
        in_specs=[vmem],
        out_specs=vmem,
        scratch_shapes=[
            pltpu.VMEM((pair_count, tile_count, local_pairs, width), part.dtype),
            pltpu.SemaphoreType.DMA((2, total)),
            pltpu.SemaphoreType.DMA,
        ],
        compiler_params=pltpu.CompilerParams(collective_id=1, has_side_effects=True),
    )(part)


def local(amplitudes, factors, pair_list, window_offsets, occupied_energy, virtual_energy):
    pair_count = lax.axis_size("pair")
    tile_count = lax.axis_size("vtile")
    row_count, col_count, aux_count = factors.shape
    window_count = window_offsets.shape[0]
    local_pairs, virt_count = (amplitudes.shape[0], amplitudes.shape[1])
    local_rows = window_offsets % row_count
    owned = (window_offsets // row_count) == lax.axis_index("vtile")
    picked = jnp.stack(
        [
            lax.dynamic_index_in_dim(factors, local_rows[slot_index], 0, keepdims=False)
            for slot_index in range(window_count)
        ]
    )
    picked = jnp.where(owned[:, None, None], picked, jnp.zeros_like(picked))
    amp = amplitudes.reshape(local_pairs, virt_count, pair_count, col_count).transpose(2, 0, 1, 3)
    arows, mine = spread(picked, amp, pair_count, tile_count)
    arows = arows.reshape(window_count, virt_count, aux_count)
    mine = mine.reshape(pair_count * local_pairs, virt_count, col_count)
    section = lax.all_gather(mine, "vtile", axis=0, tiled=True)
    integrals = jnp.einsum(
        "acq,bdq->abcd", arows, factors, preferred_element_type=jnp.float32
    ).astype(jnp.bfloat16)
    kernel = integrals.reshape(window_count * row_count, virt_count * col_count)
    flat = section.reshape(section.shape[0], virt_count * col_count)
    folded = lax.dot_general(
        flat, kernel, (((1,), (1,)), ((), ())), preferred_element_type=jnp.float32
    )
    summed = settle(
        folded.reshape(tile_count, pair_count, local_pairs, window_count * row_count)
    )
    residual = (
        summed.reshape(tile_count, local_pairs, window_count, row_count)
        .transpose(1, 2, 0, 3)
        .reshape(local_pairs, window_count, virt_count)
    )
    occupied_sum = lookup(occupied_energy, pair_list[:, 0]) + lookup(
        occupied_energy, pair_list[:, 1]
    )
    window_energy = lookup(virtual_energy, window_offsets)
    denominator = (
        window_energy[None, :, None] + virtual_energy[None, None, :] - occupied_sum[:, None, None]
    )
    update = residual / denominator
    return (residual, update)


def solution(mesh):
    return jax.shard_map(
        local,
        mesh=mesh,
        in_specs=(
            P(("pair", "vtile"), None, None),
            P("vtile", "pair", None),
            P(("pair", "vtile"), None),
            P(),
            P(),
            P(),
        ),
        out_specs=(P(("pair", "vtile"), None, None), P(("pair", "vtile"), None, None)),
        check_vma=False,
    )
```

time: 278 us -> 198 us (0.71)
  waiting for transfers between devices: 139 us -> 0.03 us
  Pallas kernels: 0 us -> 84.1 us
  blocking collectives: 27 us -> 0 us
  local copies, waits for them, and re-layouts: 8.95 us -> 33.9 us
  matrix products: 65.2 us -> 54.5 us
  other arithmetic: 13.6 us -> 5.62 us
  starting transfers between devices: 3.43 us -> 0.04 us
    pallas_call x0 -> x2, Pallas kernels: none -> 84.1 us  [the longest x1 74.7 us: spread(): pl.pallas_call(functools.partial(spread_kernel, pair_count, tile_count, s...]
    psum x1 -> x0, waiting for transfers between devices: 75.2 us -> none  [broadcast(): return lax.psum(jnp.where(mine, x, jnp.zeros_like(x)), axis)]
    all_gather x1 -> x0, waiting for transfers between devices: 54.1 us -> none  [local(): columns = lax.all_gather(picked, 'pair', axis=1, tiled=True)]
    another operation x0 -> x1, local copies, waits for them, and re-layouts: none -> 20.1 us
    unnamed x1 -> x0, blocking collectives: 16 us -> none
    all_to_all x1 -> x0, blocking collectives: 11 us -> none  [local(): lax.all_to_all(amplitudes, 'pair', split_axis=2, concat_axis=0, tiled=True)]
    dot_general x1, matrix products: 24 us -> 13.4 us  [local(): lax.dot_general(flat, kernel, (((1,), (1,)), ((), ())), preferred_element...]
    all_gather x1, waiting for transfers between devices: 7.4 us -> 0.01 us  [local(): section = lax.all_gather(mine, 'vtile', axis=0, tiled=True)]
  transfers between devices with their start and end apart: 4 -> 1, of which waited for: 4 -> 0; matrix products, arithmetic and copies ran while one was open for 19% -> 32% of each run, Pallas kernels for 0% -> 0%
where the time goes in v1:
time: 198 us; the launch traced here: 197 us
  Pallas kernels  84.1 us (42%)
  matrix products  54.5 us (28%)
  local copies, waits for them, and re-layouts  33.9 us (17%)
  between operations  19.3 us (10%)
  other arithmetic  5.62 us (3%)
    pallas_call x1, Pallas kernels, spread(): pl.pallas_call(functools.partial(spread_kernel, pair_count, tile_count, s...  74.7 us
    dot_general x1, matrix products, local(): jnp.einsum('acq,bdq->abcd', arows, factors, preferred_element_type=jnp.fl...  41.1 us
    another operation x1, local copies, waits for them, and re-layouts  20.1 us
    dot_general x1, matrix products, local(): lax.dot_general(flat, kernel, (((1,), (1,)), ((), ())), preferred_element...  13.4 us
    pallas_call x1, Pallas kernels, settle(): pl.pallas_call(functools.partial(settle_kernel, pair_count, tile_count),...  9.36 us
    dot_general x1, local copies, waits for them, and re-layouts, local(): lax.dot_general(flat, kernel, (((1,), (1,)), ((), ())), preferred_element...  7.14 us
  transfers between devices with their start and end apart: 1, of which 0 were waited for; matrix products, arithmetic and copies ran while one was open for 32% of the time, Pallas kernels for 0%

profile of v1, /device:TPU:0, one launch (start us, length us, event | category | flops | bytes accessed | tf_op | source)
XLA Modules:
  0.0 197.5 jit_solution(3037681332191733467)
XLA Ops:
  7.2 0.0 all-gather.3.cloned.1.call-start
  7.2 0.7 and_select_fusion
  7.9 0.6 fusion.9
  11.1 0.7 fusion.7
  11.7 1.3 copy.19
  13.0 0.3 copy.20
  14.6 1.3 constant_dynamic-slice_fusion.1
  15.8 0.2 maximum_select_fusion.rows_ref
  16.0 74.7 %shard_map.77 = (bf16[2,4,128,2048]{3,2,1,0:T(8,128)(2,1)S(1)}, bf16[4,1,512,128]{3,2,1,0:T(8,128)(2,1)}) custom-call(bf16[2,128,2048]{2,1,0:T(8,128)(2,1)S(1)} %maximum_select_fusion.rows_ref, bf16[4,1,512,128]{3,2,1,0:T(8,128)(2,1)S(1)} %bitcast.29), custom_call_target="tpu_custom_call" | custom-call | tf_op jit(solution)/shard_map/pallas_call | solution.py:190
  90.8 1.9 copy-done
  92.7 0.0 all-gather.3.cloned.1.call-update
  92.7 41.1 %convert_bitcast_fusion = bf16[2,64,512,128]{3,2,1,0:T(8,128)(2,1)} fusion(bf16[2,512,2048,1]{2,1,3,0:T(8,128)(2,1)} %bitcast.30, bf16[64,128,2048]{2,1,0:T(8,128)(2,1)} %param.7), kind=kOutput, calls=%fused_computation.2 | convolution fusion | flops 34368126976 | bytes 54525952 | tf_op jit(solution)/shard_map/acq,bdq->abcd/dot_general | solution.py:284
  133.9 20.1 %reshape.125 = bf16[128,65536,1]{1,0,2:T(8,128)(2,1)} reshape(bf16[2,64,512,128]{3,2,1,0:T(8,128)(2,1)} %convert_bitcast_fusion) | data formatting | bytes 33554432 | tf_op jit(solution)/shard_map/reshape.39
  154.0 0.6 fusion.8
  154.6 1.9 fusion.6
  157.8 0.2 fusion.4
  158.0 7.1 %dot_general.10 = bf16[8,4,65536]{2,1,0:T(4,128)(2,1)} reshape(bf16[32,1,512,128]{3,2,1,0:T(8,128)(2,1)} %all-gather.3.cloned.1.call-done) | data formatting | bytes 8388608 | tf_op jit(solution)/shard_map/dot_general | solution.py:289
  165.1 13.4 %fusion.10 = f32[8,4,128]{2,1,0:T(4,128)} fusion(bf16[8,4,65536]{2,1,0:T(4,128)(2,1)} %dot_general.10, bf16[128,65536,1]{1,0,2:T(8,128)(2,1)} %reshape.125), kind=kOutput, calls=%fused_computation.21 | convolution fusion | flops 536870912 | bytes 20987904 | tf_op jit(solution)/shard_map/dot_general | solution.py:289
  178.6 9.4 %shard_map.78 = f32[8,1,128]{2,1,0:T(1,128)} custom-call(f32[8,4,1,128]{3,2,1,0:T(1,128)} %bitcast.33), custom_call_target="tpu_custom_call" | custom-call | tf_op jit(solution)/shard_map/pallas_call | solution.py:250
  187.9 0.5 broadcast.92
  188.4 1.3 reduce.7
  189.8 0.1 reshape.119
  189.9 0.1 reshape.120
  189.9 0.7 subtract_divide_fusion
  (13 shorter events, 0.0 us)
Async XLA Ops:
  7.2 150.8 %all-gather.3.cloned.1.call-start = ((), (), s32[]{:S(2)}) async-start(), calls=%async_computation | async-start | bytes 4718592 | tf_op jit(solution)/shard_map/all_gather | solution.py:283
  90.7 1.9 copy-start
  133.8 20.2 %copy-start.3 = (s32[1,2]{1,0:T(1,128)S(1)}, s32[1,2]{1,0:T(1,128)}, u32[]{:S(2)}) copy-start(s32[1,2]{1,0:T(1,128)} %param.8) | copy-start | bytes 28
  133.8 20.7 %copy-start.4 = (f32[128]{0:T(128)S(1)}, f32[128]{0:T(128)}, u32[]{:S(2)}) copy-start(f32[128]{0:T(128)} %param.10) | copy-start | bytes 1540
  133.8 23.9 %copy-start.2 = (f32[512]{0:T(512)S(1)}, f32[512]{0:T(512)}, u32[]{:S(2)}) copy-start(f32[512]{0:T(512)} %param.11) | copy-start | bytes 6148
  133.8 23.9 %copy-start.5 = (s32[2]{0:T(128)S(1)}, s32[2]{0:T(128)}, u32[]{:S(2)}) copy-start(s32[2]{0:T(128)} %param.9) | copy-start | bytes 28
  189.9 0.7 copy-start.1
Sparse Core Ops, SparseCore 0:
  92.8 43.8 all-gather.2

commit v2 on v1

--- a/solution.py
+++ b/solution.py
@@ -149,13 +149,34 @@
             peer_copy(h, j).wait_recv()
             fwd_copy(h, j).start()
 
+    lower = stage < stages // 2
+    ahead, lag = 2, 3
+
+    def early(h):
+        @pl.when(lower)
+        def _():
+            go_up(h)
+
+        @pl.when(jnp.logical_not(lower))
+        def _():
+            go_down(h)
+
+    def late(h):
+        @pl.when(lower)
+        def _():
+            go_down(h)
+
+        @pl.when(jnp.logical_not(lower))
+        def _():
+            go_up(h)
+
     for h in range(count):
         combine(h)
-    lag = 3
-    for step in range(count + lag):
-        if step < count:
-            go_up(step)
-            go_down(step)
+    for step in range(-ahead, count + lag):
+        if 0 <= step + ahead < count:
+            early(step + ahead)
+        if 0 <= step < count:
+            late(step)
             finish(step)
         if step >= lag:
             forward(step - lag)
@@ -207,6 +228,52 @@
     )(picked, amp)
 
 
+def fold_kernel(amp_ref, int_ref, out_ref, amp_wide, int_wide):
+    @pl.when(pl.program_id(0) == 0)
+    def _():
+        out_ref[...] = jnp.zeros_like(out_ref)
+
+    amp_wide[...] = amp_ref[...].astype(jnp.float32)
+    int_wide[...] = int_ref[...].astype(jnp.float32)
+    total = out_ref[...]
+    for c in range(0, amp_ref.shape[1], 2):
+        left = jnp.concatenate([amp_wide[:, c, :], amp_wide[:, c + 1, :]], axis=1)
+        right = jnp.concatenate([int_wide[:, c, :], int_wide[:, c + 1, :]], axis=1)
+        total += lax.dot_general(
+            left.astype(jnp.bfloat16),
+            right.astype(jnp.bfloat16),
+            (((1,), (1,)), ((), ())),
+            preferred_element_type=jnp.float32,
+        )
+    out_ref[...] = total
+
+
+def fold(section, integrals):
+    pairs, virt, cols = section.shape
+    slots = integrals.shape[0]
+    block = 32
+    return pl.pallas_call(
+        fold_kernel,
+        grid=(virt // block,),
+        out_shape=jax.ShapeDtypeStruct((pairs, slots), jnp.float32),
+        in_specs=[
+            pl.BlockSpec((pairs, block, cols), lambda i: (0, i, 0)),
+            pl.BlockSpec((slots, block, cols), lambda i: (0, i, 0)),
+        ],
+        out_specs=pl.BlockSpec((pairs, slots), lambda i: (0, 0)),
+        scratch_shapes=[
+            pltpu.VMEM((pairs, block, cols), jnp.float32),
+            pltpu.VMEM((slots, block, cols), jnp.float32),
+        ],
+        compiler_params=pltpu.CompilerParams(vmem_limit_bytes=56 * 1024 * 1024),
+        cost_estimate=pl.CostEstimate(
+            flops=2 * pairs * slots * virt * cols,
+            bytes_accessed=2 * virt * cols * (pairs + slots),
+            transcendentals=0,
+        ),
+    )(section, integrals)
+
+
 def settle_kernel(pair_count, tile_count, part_ref, sum_ref, inbox, sems, local_sem):
     p = lax.axis_index("pair")
     t = lax.axis_index("vtile")
@@ -284,10 +351,8 @@
     integrals = jnp.einsum(
         "acq,bdq->abcd", arows, factors, preferred_element_type=jnp.float32
     ).astype(jnp.bfloat16)
-    kernel = integrals.reshape(window_count * row_count, virt_count * col_count)
-    flat = section.reshape(section.shape[0], virt_count * col_count)
-    folded = lax.dot_general(
-        flat, kernel, (((1,), (1,)), ((), ())), preferred_element_type=jnp.float32
+    folded = fold(
+        section, integrals.reshape(window_count * row_count, virt_count, col_count)
     )
     summed = settle(
         folded.reshape(tile_count, pair_count, local_pairs, window_count * row_count)

time: 198 us -> 158 us (0.80)
  local copies, waits for them, and re-layouts: 33.9 us -> 7.34 us
  matrix products: 54.5 us -> 41.5 us
    pallas_call x1, Pallas kernels: 74.7 us -> 44.4 us  [spread(): pl.pallas_call(functools.partial(spread_kernel, pair_count, tile_count, s...]
    pallas_call x0 -> x1, Pallas kernels: none -> 28.5 us  [fold(): pl.pallas_call(fold_kernel, grid=(virt // block,), out_shape=jax.ShapeDty...]
    another operation x1 -> x0, local copies, waits for them, and re-layouts: 20.1 us -> none
    dot_general x1 -> x0, matrix products: 13.4 us -> none  [local(): lax.dot_general(flat, kernel, (((1,), (1,)), ((), ())), preferred_element...]
    dot_general x1 -> x0, local copies, waits for them, and re-layouts: 7.14 us -> none  [local(): lax.dot_general(flat, kernel, (((1,), (1,)), ((), ())), preferred_element...]
  transfers between devices with their start and end apart: 1 -> 1, of which waited for: 0 -> 0; matrix products, arithmetic and copies ran while one was open for 32% -> 29% of each run, Pallas kernels for 0% -> 0%
where the time goes in v2:
time: 158 us; the launch traced here: 157 us
  Pallas kernels  82.3 us (52%)
  matrix products  41.5 us (26%)
  between operations  19.2 us (12%)
  local copies, waits for them, and re-layouts  7.34 us (5%)
  other arithmetic  7.04 us (4%)
    pallas_call x1, Pallas kernels, spread(): pl.pallas_call(functools.partial(spread_kernel, pair_count, tile_count, s...  44.4 us
    dot_general x1, matrix products, local(): jnp.einsum('acq,bdq->abcd', arows, factors, preferred_element_type=jnp.fl...  41.5 us
    pallas_call x1, Pallas kernels, fold(): pl.pallas_call(fold_kernel, grid=(virt // block,), out_shape=jax.ShapeDty...  28.5 us
    pallas_call x1, Pallas kernels, settle(): pl.pallas_call(functools.partial(settle_kernel, pair_count, tile_count),...  9.36 us
    reduce_sum x2, other arithmetic, lookup(): jnp.sum(jnp.where(positions[None, :] == indices[:, None], table[None, :],...  3.52 us
    unnamed x7, local copies, waits for them, and re-layouts  3.22 us
  transfers between devices with their start and end apart: 1, of which 0 were waited for; matrix products, arithmetic and copies ran while one was open for 29% of the time, Pallas kernels for 0%

profile of v2, /device:TPU:0, one launch (start us, length us, event | category | flops | bytes accessed | tf_op | source)
XLA Modules:
  0.0 157.4 jit_solution(556839585252537726)
XLA Ops:
  7.2 0.0 all-gather.3.cloned.1.call-start
  7.2 0.7 and_select_fusion
  7.9 0.6 fusion.10
  11.1 0.7 fusion.8
  11.7 1.3 copy.17
  13.0 0.3 copy.18
  14.6 1.3 constant_dynamic-slice_fusion.1
  15.8 0.2 maximum_select_fusion.rows_ref
  16.0 44.4 %shard_map.77 = (bf16[2,4,128,2048]{3,2,1,0:T(8,128)(2,1)S(1)}, bf16[4,1,512,128]{3,2,1,0:T(8,128)(2,1)}) custom-call(bf16[2,128,2048]{2,1,0:T(8,128)(2,1)S(1)} %maximum_select_fusion.rows_ref, bf16[4,1,512,128]{3,2,1,0:T(8,128)(2,1)S(1)} %bitcast.25), custom_call_target="tpu_custom_call" | custom-call | tf_op jit(solution)/shard_map/pallas_call | solution.py:211
  60.4 0.0 copy-start
  60.4 2.0 %copy-done = bf16[2,4,128,2048]{3,2,1,0:T(8,128)(2,1)} copy-done((bf16[2,4,128,2048]{3,2,1,0:T(8,128)(2,1)}, bf16[2,4,128,2048]{3,2,1,0:T(8,128)(2,1)S(1)}, u32[]{:S(2)}) %copy-start) | copy-done | bytes 4194328
  62.4 0.0 all-gather.3.cloned.1.call-update
  62.4 1.3 fusion.9
  63.7 2.6 %fusion.7 = (f32[]{:T(128)}, f32[]{:T(128)}) fusion(f32[128]{0:T(128)} %param.10, s32[]{:T(128)} %bitcast.14, s32[]{:T(128)} %bitcast.13), kind=kLoop, calls=%fused_computation.15 | loop fusion | flops 766 | bytes 528 | tf_op jit(solution)/shard_map/reduce_sum | solution.py:15
  67.6 0.9 fusion.5
  68.5 41.5 %fusion.2 = bf16[2,512,64,128]{3,1,2,0:T(8,128)(2,1)} fusion(bf16[2,512,2048,1]{2,1,3,0:T(8,128)(2,1)} %bitcast.26, bf16[64,128,2048]{2,1,0:T(8,128)(2,1)} %param.7), kind=kOutput, calls=%fused_computation.2 | convolution fusion | flops 34368126976 | bytes 54525952 | tf_op jit(solution)/shard_map/acq,bdq->abcd/dot_general | solution.py:351
  110.0 28.5 %shard_map.78 = f32[32,128]{1,0:T(8,128)} custom-call(bf16[32,512,128]{2,1,0:T(8,128)(2,1)} %bitcast.28, bf16[128,512,128]{2,1,0:T(8,128)(2,1)} %bitcast.27), custom_call_target="tpu_custom_call" | custom-call | flops 536870912 | bytes 20971520 | tf_op jit(solution)/shard_map/pallas_call | solution.py:255
  138.5 9.4 %shard_map.79 = f32[8,1,128]{2,1,0:T(1,128)} custom-call(f32[8,4,1,128]{3,2,1,0:T(1,128)} %bitcast.30), custom_call_target="tpu_custom_call" | custom-call | tf_op jit(solution)/shard_map/pallas_call | solution.py:317
  147.9 0.5 broadcast.92
  148.4 1.3 reduce.7
  149.7 0.1 reshape.114
  149.8 0.1 reshape.115
  149.9 0.7 subtract_divide_fusion
  150.6 0.0 copy-done.1
  (5 shorter events, 0.0 us)
Async XLA Ops:
  7.2 102.8 %all-gather.3.cloned.1.call-start = ((), (), s32[]{:S(2)}) async-start(), calls=%async_computation | async-start | bytes 4718592 | tf_op jit(solution)/shard_map/all_gather | solution.py:350
  60.4 2.0 %copy-start = (bf16[2,4,128,2048]{3,2,1,0:T(8,128)(2,1)}, bf16[2,4,128,2048]{3,2,1,0:T(8,128)(2,1)S(1)}, u32[]{:S(2)}) copy-start(bf16[2,4,128,2048]{3,2,1,0:T(8,128)(2,1)S(1)} %get-tuple-element.5) | copy-start | bytes 12582916
  109.9 39.9 %copy-start.2 = (f32[512]{0:T(512)S(1)}, f32[512]{0:T(512)}, u32[]{:S(2)}) copy-start(f32[512]{0:T(512)} %param.11) | copy-start | bytes 6148
  149.9 0.7 copy-start.1
Sparse Core Ops, SparseCore 0:
  62.5 45.4 all-gather.2

commit v3 on v2

--- a/solution.py
+++ b/solution.py
@@ -31,8 +31,16 @@
     mate = (p, stage * 2 + (1 - core))
     above = (p, t + 2)
     below = (p, t - 2)
-    peers = [(lax.rem(p + j, pair_count), t) for j in range(1, pair_count)]
-    sources = [lax.rem(p + pair_count - j, pair_count) for j in range(1, pair_count)]
+    relayed = pair_count == 4
+    if relayed:
+        across = p + 1 - 2 * lax.rem(p, 2)
+        along = lax.rem(p + 2, 4)
+        sources = [across, along, lax.rem(across + 2, 4)]
+        peers = [(source, t) for source in sources]
+    else:
+        peers = [(lax.rem(p + j, pair_count), t) for j in range(1, pair_count)]
+        sources = [lax.rem(p + pair_count - j, pair_count) for j in range(1, pair_count)]
+    near = 2 if relayed else pair_count - 1
 
     barrier = pltpu.get_barrier_semaphore()
     around = [(p, lax.rem(t + 2, tile_count)), (p, lax.rem(t + tile_count - 2, tile_count))]
@@ -65,6 +73,9 @@
 
     def peer_copy(h, j):
         k, rows = chunks[h]
+        if j >= near:
+            place = full_ref.at[k, sources[h % 2], rows, mine_lanes]
+            return remote(place, place, peer_sems, (j, h), peers[1 - h % 2])
         place = full_ref.at[k, p, rows, mine_lanes]
         return remote(place, place, peer_sems, (j, h), peers[j])
 
@@ -140,14 +151,21 @@
                 own_buf[k, rows, :] + up_buf[k, rows, :] + down_buf[k, rows, :]
             )
 
-        for j in range(pair_count - 1):
+        for j in range(near):
             peer_copy(h, j).start()
         fwd_copy(h, pair_count - 1).start()
 
     def forward(h):
-        for j in range(pair_count - 1):
+        for j in range(near):
             peer_copy(h, j).wait_recv()
             fwd_copy(h, j).start()
+            if relayed and j == h % 2:
+                peer_copy(h, near).start()
+
+    def forward_far(h):
+        for j in range(near, pair_count - 1):
+            peer_copy(h, j).wait_recv()
+            fwd_copy(h, j).start()
 
     lower = stage < stages // 2
     ahead, lag = 2, 3
@@ -172,14 +190,16 @@
 
     for h in range(count):
         combine(h)
-    for step in range(-ahead, count + lag):
+    for step in range(-ahead, count + 2 * lag):
         if 0 <= step + ahead < count:
             early(step + ahead)
         if 0 <= step < count:
             late(step)
             finish(step)
-        if step >= lag:
+        if 0 <= step - lag < count:
             forward(step - lag)
+        if 0 <= step - 2 * lag < count:
+            forward_far(step - 2 * lag)
     for h in range(count):
         core_copy(h).wait_send()
 
@@ -228,22 +248,18 @@
     )(picked, amp)
 
 
-def fold_kernel(amp_ref, int_ref, out_ref, amp_wide, int_wide):
+def fold_kernel(amp_ref, int_ref, out_ref):
     @pl.when(pl.program_id(0) == 0)
     def _():
         out_ref[...] = jnp.zeros_like(out_ref)
 
-    amp_wide[...] = amp_ref[...].astype(jnp.float32)
-    int_wide[...] = int_ref[...].astype(jnp.float32)
+    pairs, block, cols = amp_ref.shape
     total = out_ref[...]
-    for c in range(0, amp_ref.shape[1], 2):
-        left = jnp.concatenate([amp_wide[:, c, :], amp_wide[:, c + 1, :]], axis=1)
-        right = jnp.concatenate([int_wide[:, c, :], int_wide[:, c + 1, :]], axis=1)
+    for c in range(0, block, 16):
+        left = amp_ref[:, c : c + 16, :].reshape(pairs, 16 * cols)
+        right = int_ref[:, c : c + 16, :].reshape(int_ref.shape[0], 16 * cols)
         total += lax.dot_general(
-            left.astype(jnp.bfloat16),
-            right.astype(jnp.bfloat16),
-            (((1,), (1,)), ((), ())),
-            preferred_element_type=jnp.float32,
+            left, right, (((1,), (1,)), ((), ())), preferred_element_type=jnp.float32
         )
     out_ref[...] = total
 
@@ -251,7 +267,7 @@
 def fold(section, integrals):
     pairs, virt, cols = section.shape
     slots = integrals.shape[0]
-    block = 32
+    block = 64
     return pl.pallas_call(
         fold_kernel,
         grid=(virt // block,),
@@ -261,10 +277,6 @@
             pl.BlockSpec((slots, block, cols), lambda i: (0, i, 0)),
         ],
         out_specs=pl.BlockSpec((pairs, slots), lambda i: (0, 0)),
-        scratch_shapes=[
-            pltpu.VMEM((pairs, block, cols), jnp.float32),
-            pltpu.VMEM((slots, block, cols), jnp.float32),
-        ],
         compiler_params=pltpu.CompilerParams(vmem_limit_bytes=56 * 1024 * 1024),
         cost_estimate=pl.CostEstimate(
             flops=2 * pairs * slots * virt * cols,

time: 158 us -> 139 us (0.88)
  Pallas kernels: 82.3 us -> 63 us
    pallas_call x1, Pallas kernels: 28.5 us -> 13.6 us  [fold(): pl.pallas_call(fold_kernel, grid=(virt // block,), out_shape=jax.ShapeDty...]
    pallas_call x1, Pallas kernels: 44.4 us -> 40.1 us  [spread(): pl.pallas_call(functools.partial(spread_kernel, pair_count, tile_count, s...]
  transfers between devices with their start and end apart: 1 -> 1, of which waited for: 0 -> 0; matrix products, arithmetic and copies ran while one was open for 29% -> 34% of each run, Pallas kernels for 0% -> 0%
where the time goes in v3:
time: 139 us; the launch traced here: 138 us
  Pallas kernels  63 us (45%)
  matrix products  41.5 us (30%)
  between operations  19.2 us (14%)
  local copies, waits for them, and re-layouts  7.34 us (5%)
  other arithmetic  7.04 us (5%)
    dot_general x1, matrix products, local(): jnp.einsum('acq,bdq->abcd', arows, factors, preferred_element_type=jnp.fl...  41.5 us
    pallas_call x1, Pallas kernels, spread(): pl.pallas_call(functools.partial(spread_kernel, pair_count, tile_count, s...  40.1 us
    pallas_call x1, Pallas kernels, fold(): pl.pallas_call(fold_kernel, grid=(virt // block,), out_shape=jax.ShapeDty...  13.6 us
    pallas_call x1, Pallas kernels, settle(): pl.pallas_call(functools.partial(settle_kernel, pair_count, tile_count),...  9.36 us
    reduce_sum x2, other arithmetic, lookup(): jnp.sum(jnp.where(positions[None, :] == indices[:, None], table[None, :],...  3.52 us
    unnamed x7, local copies, waits for them, and re-layouts  3.22 us
  transfers between devices with their start and end apart: 1, of which 0 were waited for; matrix products, arithmetic and copies ran while one was open for 34% of the time, Pallas kernels for 0%

profile of v3, /device:TPU:0, one launch (start us, length us, event | category | flops | bytes accessed | tf_op | source)
XLA Modules:
  0.0 138.2 jit_solution(9495174075067089906)
XLA Ops:
  7.2 0.0 all-gather.3.cloned.1.call-start
  7.2 0.7 and_select_fusion
  7.9 0.6 fusion.10
  11.1 0.7 fusion.8
  11.7 1.3 copy.17
  13.0 0.3 copy.18
  14.6 1.3 constant_dynamic-slice_fusion.1
  15.8 0.2 maximum_select_fusion.rows_ref
  16.0 40.1 %shard_map.77 = (bf16[2,4,128,2048]{3,2,1,0:T(8,128)(2,1)S(1)}, bf16[4,1,512,128]{3,2,1,0:T(8,128)(2,1)}) custom-call(bf16[2,128,2048]{2,1,0:T(8,128)(2,1)S(1)} %maximum_select_fusion.rows_ref, bf16[4,1,512,128]{3,2,1,0:T(8,128)(2,1)S(1)} %bitcast.25), custom_call_target="tpu_custom_call" | custom-call | tf_op jit(solution)/shard_map/pallas_call | solution.py:231
  56.1 0.0 copy-start
  56.1 2.0 %copy-done = bf16[2,4,128,2048]{3,2,1,0:T(8,128)(2,1)} copy-done((bf16[2,4,128,2048]{3,2,1,0:T(8,128)(2,1)}, bf16[2,4,128,2048]{3,2,1,0:T(8,128)(2,1)S(1)}, u32[]{:S(2)}) %copy-start) | copy-done | bytes 4194328
  58.1 0.0 all-gather.3.cloned.1.call-update
  58.1 1.3 fusion.9
  59.4 2.6 %fusion.7 = (f32[]{:T(128)}, f32[]{:T(128)}) fusion(f32[128]{0:T(128)} %param.10, s32[]{:T(128)} %bitcast.14, s32[]{:T(128)} %bitcast.13), kind=kLoop, calls=%fused_computation.15 | loop fusion | flops 766 | bytes 528 | tf_op jit(solution)/shard_map/reduce_sum | solution.py:15
  63.3 0.9 fusion.5
  64.2 41.5 %fusion.2 = bf16[2,512,64,128]{3,1,2,0:T(8,128)(2,1)} fusion(bf16[2,512,2048,1]{2,1,3,0:T(8,128)(2,1)} %bitcast.26, bf16[64,128,2048]{2,1,0:T(8,128)(2,1)} %param.7), kind=kOutput, calls=%fused_computation.2 | convolution fusion | flops 34368126976 | bytes 54525952 | tf_op jit(solution)/shard_map/acq,bdq->abcd/dot_general | solution.py:363
  105.7 13.6 %shard_map.78 = f32[32,128]{1,0:T(8,128)} custom-call(bf16[32,512,128]{2,1,0:T(8,128)(2,1)} %bitcast.28, bf16[128,512,128]{2,1,0:T(8,128)(2,1)} %bitcast.27), custom_call_target="tpu_custom_call" | custom-call | flops 536870912 | bytes 20971520 | tf_op jit(solution)/shard_map/pallas_call | solution.py:271
  119.3 9.4 %shard_map.79 = f32[8,1,128]{2,1,0:T(1,128)} custom-call(f32[8,4,1,128]{3,2,1,0:T(1,128)} %bitcast.30), custom_call_target="tpu_custom_call" | custom-call | tf_op jit(solution)/shard_map/pallas_call | solution.py:329
  128.7 0.5 broadcast.92
  129.2 1.3 reduce.7
  130.5 0.1 reshape.114
  130.6 0.1 reshape.115
  130.7 0.0 copy-done.2
  130.7 0.7 subtract_divide_fusion
  (5 shorter events, 0.0 us)
Async XLA Ops:
  7.2 98.5 %all-gather.3.cloned.1.call-start = ((), (), s32[]{:S(2)}) async-start(), calls=%async_computation | async-start | bytes 4718592 | tf_op jit(solution)/shard_map/all_gather | solution.py:362
  56.1 2.0 %copy-start = (bf16[2,4,128,2048]{3,2,1,0:T(8,128)(2,1)}, bf16[2,4,128,2048]{3,2,1,0:T(8,128)(2,1)S(1)}, u32[]{:S(2)}) copy-start(bf16[2,4,128,2048]{3,2,1,0:T(8,128)(2,1)S(1)} %get-tuple-element.5) | copy-start | bytes 12582916
  105.7 25.0 %copy-start.2 = (f32[512]{0:T(512)S(1)}, f32[512]{0:T(512)}, u32[]{:S(2)}) copy-start(f32[512]{0:T(512)} %param.11) | copy-start | bytes 6148
  130.7 0.7 copy-start.1
Sparse Core Ops, SparseCore 0:
  58.2 45.8 all-gather.2
